TPU v7x, 128 devices: a whole 4x4x4 slice. The times are simulated.
128 devices in a mesh: req: 16 (over x, z), head: 8 (over y, core).
Axes of the slice: x: 4, y: 4, z: 4, core: 2. Of those that a mesh axis runs over, the one named last changes fastest.
Arguments:
- hidden: bfloat16 [512, 2048], P('req', 'head'), may hold values from -6 to 6
- lengths: int32 [512], P('req'), may hold values from 1 to 384, as said below
- expert_ids: int32 [512, 8], P('req'), may hold values from 0 to 63, all different within a row
- route_weights: float32 [512, 8], P('req'), may hold values from 0.25 to 2.5
- w_qkv: bfloat16 [3, 2048, 2048], P(None, None, 'head'), may hold values from -0.125 to 0.125
- w_out: bfloat16 [2048, 2048], P('head'), may hold values from -0.125 to 0.125
- k_cache: bfloat16 [512, 384, 16, 128], P('req', None, 'head'), may hold values from -400 to 400
- v_cache: bfloat16 [512, 384, 16, 128], P('req', None, 'head'), may hold values from -12 to 12
- w_in: bfloat16 [2048, 64, 2048], P(None, 'head', 'req'), may hold values from -0.125 to 0.125
- w_down: bfloat16 [64, 1024, 2048], P('head', 'req'), may hold values from -0.1875 to 0.1875
Outputs:
- output: bfloat16 [512, 2048], P('req', 'head')
Inputs may be any that keep to these rules, and one draw needn't show every extreme that they name: `lengths`: some request has exactly 384 cached positions.
All inputs are finite; a program needn't handle non-finite values.
Results may differ from a plain program's by a relative error of at most 0.023.
Values may be sent and summed in bfloat16 or wider, within the bound.
A program may use at most 128 MiB of HBM per device.

v0:
```python
import jax
import jax.numpy as jnp
from jax import lax
from jax.sharding import PartitionSpec as P

UNIT_BLOCK = 64
KEY_BLOCK = 128


rope_theta = 50000.0
norm_eps = 1e-05


def over_all(shard, axis, dim, work):
    return work(lax.all_gather(shard, axis, axis=dim, tiled=True), jnp.int32(0))


def rotate(values, positions):
    half_dim = values.shape[-1] // 2
    freqs = rope_theta ** (-jnp.arange(half_dim, dtype=jnp.float32) / half_dim)
    angles = positions.astype(jnp.float32)[:, None] * freqs[None, :]
    cosine = jnp.cos(angles)[:, None, :]
    sine = jnp.sin(angles)[:, None, :]
    first_half = values[..., :half_dim]
    second_half = values[..., half_dim:]
    return jnp.concatenate(
        [first_half * cosine - second_half * sine, second_half * cosine + first_half * sine],
        axis=-1,
    )


def rms_normed(values):
    return (
        values * lax.rsqrt(jnp.mean(values * values, axis=-1, keepdims=True) + norm_eps)
    ).astype(jnp.bfloat16)


def per_device(
    hidden, lengths, expert_ids, route_weights, w_qkv, w_out, k_cache, v_cache, w_in, w_down
):
    full_rows = lax.all_gather(hidden, "head", axis=1, tiled=True)
    hidden_f = full_rows.astype(jnp.float32)
    normed = rms_normed(hidden_f)
    req_local = hidden.shape[0]
    col_width = hidden.shape[1]
    heads_local = k_cache.shape[2]
    head_size = k_cache.shape[3]
    cache_len = k_cache.shape[1]
    projected = jnp.einsum("td,cdn->ctn", normed, w_qkv, preferred_element_type=jnp.float32)
    projected = projected.reshape(3, req_local, heads_local, head_size)
    query = rotate(projected[0], lengths).astype(jnp.bfloat16)
    key_new = rotate(projected[1], lengths).astype(jnp.bfloat16)
    value_new = projected[2].astype(jnp.bfloat16)
    score_scale = head_size ** (-0.5)
    block_count = (jnp.max(lengths) + KEY_BLOCK - 1) // KEY_BLOCK

    def score_block(block_idx, buffer):
        keys_block = lax.dynamic_slice_in_dim(k_cache, block_idx * KEY_BLOCK, KEY_BLOCK, 1)
        block_scores = (
            jnp.einsum("rhd,rlhd->rhl", query, keys_block, preferred_element_type=jnp.float32)
            * score_scale
        )
        return lax.dynamic_update_slice_in_dim(buffer, block_scores, block_idx * KEY_BLOCK, 2)

    buffer = jnp.full((req_local, heads_local, cache_len), -jnp.inf, jnp.float32)
    buffer = lax.fori_loop(0, block_count, score_block, buffer)
    positions = jnp.arange(cache_len, dtype=jnp.int32)
    scores = jnp.where(positions[None, None, :] < lengths[:, None, None], buffer, -jnp.inf)
    self_score = (
        jnp.einsum("rhd,rhd->rh", query, key_new, preferred_element_type=jnp.float32) * score_scale
    )
    row_top = jnp.maximum(jnp.max(scores, axis=-1), self_score)
    exponent = jnp.exp(scores - row_top[:, :, None])
    self_exp = jnp.exp(self_score - row_top)
    denominator = jnp.sum(exponent, axis=-1) + self_exp
    weights = (exponent / denominator[:, :, None]).astype(jnp.bfloat16)
    self_weight = (self_exp / denominator).astype(jnp.bfloat16)

    def value_block(block_idx, accum):
        weights_block = lax.dynamic_slice_in_dim(weights, block_idx * KEY_BLOCK, KEY_BLOCK, 2)
        values_block = lax.dynamic_slice_in_dim(v_cache, block_idx * KEY_BLOCK, KEY_BLOCK, 1)
        return accum + jnp.einsum(
            "rhl,rlhd->rhd", weights_block, values_block, preferred_element_type=jnp.float32
        )

    accum = lax.fori_loop(
        0, block_count, value_block, jnp.zeros((req_local, heads_local, head_size), jnp.float32)
    )
    accum = accum + self_weight.astype(jnp.float32)[:, :, None] * value_new.astype(jnp.float32)
    attended = accum.astype(jnp.bfloat16).reshape(req_local, heads_local * head_size)
    head_terms = jnp.dot(attended, w_out, preferred_element_type=jnp.float32)
    resid = hidden_f + lax.psum(head_terms.astype(jnp.bfloat16), "head").astype(jnp.float32)
    mixed = rms_normed(resid)
    experts_local = w_down.shape[0]
    units_local = w_down.shape[1]
    width = w_in.shape[0]
    expert_base = lax.axis_index("head") * experts_local + jnp.arange(
        experts_local, dtype=jnp.int32
    )
    w_in_flat = w_in.reshape(width, experts_local * 2 * units_local)
    w_down_flat = w_down.reshape(experts_local * units_local, width)

    def expert_hidden(pieces):
        token_rows, token_ids, token_weights = pieces
        row_count = token_rows.shape[0]
        matches = (token_ids[:, :, None] == expert_base[None, None, :]).astype(jnp.float32)
        combined = jnp.sum(token_weights[:, :, None] * matches, axis=1)
        gate_up = jnp.dot(token_rows, w_in_flat, preferred_element_type=jnp.float32)
        gate_up = gate_up.reshape(
            row_count, experts_local, units_local // UNIT_BLOCK, 2, UNIT_BLOCK
        )
        gate = gate_up[:, :, :, 0, :]
        upward = gate_up[:, :, :, 1, :]
        units = (combined[:, :, None, None] * (jax.nn.silu(gate) * upward)).astype(jnp.bfloat16)
        return units.reshape(row_count, experts_local * units_local)

    gathered = over_all(
        (mixed, expert_ids, route_weights.astype(jnp.bfloat16)),
        "req",
        0,
        lambda piece, start: expert_hidden((piece[0], piece[1], piece[2].astype(jnp.float32))),
    )
    token_sums = lax.psum_scatter(
        jnp.dot(gathered, w_down_flat, preferred_element_type=jnp.float32).astype(jnp.bfloat16),
        "req",
        scatter_dimension=0,
        tiled=True,
    )
    moe_share = lax.psum_scatter(token_sums, "head", scatter_dimension=1, tiled=True).astype(
        jnp.float32
    )
    resid_share = lax.dynamic_slice_in_dim(resid, lax.axis_index("head") * col_width, col_width, 1)
    return (resid_share + moe_share).astype(jnp.bfloat16)


def solution(mesh):
    in_specs = (
        P("req", "head"),
        P("req"),
        P("req", None),
        P("req", None),
        P(None, None, "head"),
        P("head", None),
        P("req", None, "head", None),
        P("req", None, "head", None),
        P(None, "head", "req"),
        P("head", "req", None),
    )
    out_specs = P("req", "head")
    return jax.shard_map(
        per_device, mesh=mesh, in_specs=in_specs, out_specs=out_specs, check_vma=False
    )
```

profile of v0, /device:TPU:0, one launch (start us, length us, event | category | flops | bytes accessed | tf_op | source)
XLA Modules:
  0.0 295.3 jit_solution(10941780529254591769)
XLA Ops:
  6.5 0.0 copy-start
  6.5 0.0 all-reduce.2.cloned.1.call-start
  6.5 1.5 fusion.28
  8.8 0.7 iota_compare_fusion
  9.5 13.6 %all_gather.12 = bf16[32,2048]{1,0:T(8,128)(2,1)S(1)} all-gather(bf16[32,256]{1,0:T(8,128)(2,1)} %param.14), channel_id=1, replica_groups=mesh['req'=16,'head'=8] {'head'}, dimensions={1}, use_global_device_ids=true | all-gather | bytes 147456 | tf_op jit(solution)/shard_map/all_gather | solution.py:41
  23.1 0.1 fusion.14
  23.3 0.0 copy-done
  23.3 0.7 convolution_bitcast_fusion
  24.1 0.1 multiply_cosine_fusion
  24.2 0.2 subtract_convert_fusion.1
  24.4 0.2 fusion.20
  24.6 13.6 %while.20 = (s32[]{:T(128)}, f32[32,2,384]{2,1,0:T(2,128)S(1)}, s32[]{:T(128)}, bf16[32,384,2,128]{3,2,1,0:T(2,128)(2,1)}, bf16[32,2,128]{2,1,0:T(2,128)(2,1)S(1...) while((s32[]{:T(128)}, f32[32,2,384]{2,1,0:T(2,128)S(1)}, s32[]{:T(128)}, ...), condition=%wide.region_3.4_spmd, body=%wide.region_2.3_spmd.sunk | while | flops 2105350 | bytes 6406299 | solution.py:66
  24.6 3.3 %constant_dynamic-slice_fusion.4 = bf16[32,128,2,128]{3,2,1,0:T(2,128)(2,1)S(1)} fusion(bf16[32,384,2,128]{3,2,1,0:T(2,128)(2,1)} %get-tuple-element.186, s32[]{:T(128)S(6)} %select_n.34), kind=kLoop, calls=%fused_computation.4.clone.1 | loop fusion | bytes 4194308 | tf_op jit(solution)/shard_map/while/body/dynamic_slice | solution.py:58
  27.9 1.2 fusion.42
  29.1 0.1 multiply_dynamic-update-slice_fusion.2
  29.2 3.3 %constant_dynamic-slice_fusion.4 = bf16[32,128,2,128]{3,2,1,0:T(2,128)(2,1)S(1)} fusion(bf16[32,384,2,128]{3,2,1,0:T(2,128)(2,1)} %get-tuple-element.186, s32[]{:T(128)S(6)} %select_n.34), kind=kLoop, calls=%fused_computation.4.clone.1 | loop fusion | bytes 4194308 | tf_op jit(solution)/shard_map/while/body/dynamic_slice | solution.py:58
  32.5 1.2 fusion.42
  33.6 0.1 multiply_dynamic-update-slice_fusion.2
  33.7 3.3 %constant_dynamic-slice_fusion.4 = bf16[32,128,2,128]{3,2,1,0:T(2,128)(2,1)S(1)} fusion(bf16[32,384,2,128]{3,2,1,0:T(2,128)(2,1)} %get-tuple-element.186, s32[]{:T(128)S(6)} %select_n.34), kind=kLoop, calls=%fused_computation.4.clone.1 | loop fusion | bytes 4194308 | tf_op jit(solution)/shard_map/while/body/dynamic_slice | solution.py:58
  37.0 1.2 fusion.42
  38.2 0.1 multiply_dynamic-update-slice_fusion.2
  38.2 0.1 fusion.19
  38.4 0.2 fusion.24
  38.6 0.2 divide_convert_fusion
  38.9 12.1 %while.21 = (s32[]{:T(128)}, f32[32,2,128]{2,1,0:T(2,128)S(1)}, s32[]{:T(128)}, bf16[32,2,384]{2,1,0:T(2,128)(2,1)S(1)}, bf16[32,384,2,128]{3,2,1,0:T(2,128)(2,1...) while((s32[]{:T(128)}, f32[32,2,128]{2,1,0:T(2,128)S(1)}, s32[]{:T(128)}, ...), condition=%wide.region_7.8_spmd, body=%wide.region_6.7_spmd.sunk | while | flops 2105350 | bytes 6471835 | solution.py:86
  38.9 3.3 %constant_dynamic-slice_fusion.5 = bf16[32,128,2,128]{3,2,1,0:T(2,128)(2,1)S(1)} fusion(bf16[32,384,2,128]{3,2,1,0:T(2,128)(2,1)} %get-tuple-element.214, s32[]{:T(128)S(6)} %select_n.35), kind=kLoop, calls=%fused_computation.9.clone.1 | loop fusion | bytes 4194308 | tf_op jit(solution)/shard_map/while/body/dynamic_slice | solution.py:81
  42.2 0.6 fusion.45
  42.9 3.3 %constant_dynamic-slice_fusion.5 = bf16[32,128,2,128]{3,2,1,0:T(2,128)(2,1)S(1)} fusion(bf16[32,384,2,128]{3,2,1,0:T(2,128)(2,1)} %get-tuple-element.214, s32[]{:T(128)S(6)} %select_n.35), kind=kLoop, calls=%fused_computation.9.clone.1 | loop fusion | bytes 4194308 | tf_op jit(solution)/shard_map/while/body/dynamic_slice | solution.py:81
  46.2 0.6 fusion.45
  46.9 3.3 %constant_dynamic-slice_fusion.5 = bf16[32,128,2,128]{3,2,1,0:T(2,128)(2,1)S(1)} fusion(bf16[32,384,2,128]{3,2,1,0:T(2,128)(2,1)} %get-tuple-element.214, s32[]{:T(128)S(6)} %select_n.35), kind=kLoop, calls=%fused_computation.9.clone.1 | loop fusion | bytes 4194308 | tf_op jit(solution)/shard_map/while/body/dynamic_slice | solution.py:81
  50.2 0.6 fusion.45
  51.0 0.1 add_convert_fusion.1
  51.1 2.2 convolution_convert_fusion.1
  53.2 0.0 all-reduce.2.cloned.1.call-update
  53.3 0.0 all-gather.4.cloned.1.call-start
  53.3 60.9 %all-reduce.2.cloned.1.call-done = bf16[32,2048]{1,0:T(8,128)(2,1)} async-done(((bf16[32,2048]{1,0:T(8,128)(2,1)}), bf16[32,2048]{1,0:T(8,128)(2,1)}) %all-reduce.2.cloned.1.call-update) | async-done | bytes 131088 | tf_op jit(solution)/shard_map/psum | solution.py:92
  114.3 1.1 convert_add_fusion
  115.3 1.6 multiply_convert_fusion
  117.0 0.0 all-gather.4.cloned.1.call-update
  117.0 0.0 reduce-scatter.3.cloned.1.call-start
  117.0 5.3 %copy.57 = bf16[256,8,8,128]{3,1,2,0:T(8,128)(2,1)} copy(bf16[256,8,8,128]{3,2,1,0:T(8,128)(2,1)} %bitcast.70) | data formatting | bytes 8388608
  122.3 0.0 copy-start.1
  122.3 6.5 %copy.27 = bf16[1024,2048]{1,0:T(8,128)(2,1)} copy(bf16[1024,2048]{0,1:T(8,128)(2,1)} %bitcast.69) | data formatting | bytes 8388608 | tf_op jit(solution)/shard_map/dot_general | solution.py:108
  128.8 0.0 copy-done.1
  128.8 23.5 %all-gather.1 = bf16[16,32,8]{1,2,0:T(8,128)(2,1)S(1)} all-gather(bf16[1,32,8]{1,2,0:T(8,128)(2,1)S(1)} %convert_bitcast_fusion), channel_id=1, replica_groups=mesh['req'=16,'head'=8] {'req'}, dimensions={0}, use_global_device_ids=true | all-gather | bytes 8704 | tf_op jit(solution)/shard_map/all_gather | solution.py:15
  152.3 0.1 reshape.224
  152.4 23.1 %all-gather = s32[16,32,8]{1,2,0:T(8,128)S(1)} all-gather(s32[1,32,8]{1,2,0:T(8,128)} %bitcast.77), channel_id=1, replica_groups=mesh['req'=16,'head'=8] {'req'}, dimensions={0}, use_global_device_ids=true | all-gather | bytes 17408 | tf_op jit(solution)/shard_map/all_gather | solution.py:15
  175.6 0.1 reshape.221
  175.7 0.1 select_reduce_fusion
  175.8 0.0 all-gather.4.cloned.1.call-done
  175.8 5.2 %fusion.8 = f32[512,8,1,2,64]{0,4,3,1,2:T(8,128)S(1)} fusion(bf16[8,2,64,2048]{3,2,1,0:T(8,128)(2,1)} %bitcast.71, bf16[512,2048]{1,0:T(8,128)(2,1)} %all-gather.4.cloned.1.call-done), kind=kOutput, calls=%fused_computation.15 | convolution fusion | flops 2147483648 | bytes 8388608 | tf_op jit(solution)/shard_map/dot_general | solution.py:108
  181.0 0.0 copy-start.2
  181.0 0.3 fusion.13
  181.3 1.2 copy-done.2
  182.6 2.6 convolution_convert_fusion
  185.2 0.0 reduce-scatter.3.cloned.1.call-update
  185.2 0.0 reduce-scatter.5.cloned.1.call-start
  185.3 70.5 %reduce-scatter.3.cloned.1.call-done = bf16[32,2048]{1,0:T(8,128)(2,1)} async-done(((bf16[512,2048]{1,0:T(8,128)(2,1)}), bf16[32,2048]{1,0:T(8,128)(2,1)}) %reduce-scatter.3.cloned.1.call-update) | async-done | bytes 131088 | tf_op jit(solution)/shard_map/reduce_scatter | solution.py:123
  255.8 0.0 reduce-scatter.5.cloned.1.call-update
  255.8 31.7 %reduce-scatter.5.cloned.1.call-done = bf16[32,256]{1,0:T(8,128)(2,1)} async-done(((bf16[32,2048]{1,0:T(8,128)(2,1)}), bf16[32,256]{1,0:T(8,128)(2,1)}) %reduce-scatter.5.cloned.1.call-update) | async-done | bytes 16400 | tf_op jit(solution)/shard_map/reduce_scatter | solution.py:129
  287.5 1.3 add_convert_fusion
  (22 shorter events, 0.4 us)
Async XLA Ops:
  6.5 16.7 %copy-start = (bf16[3,2048,256]{2,1,0:T(8,128)(2,1)S(1)}, bf16[3,2048,256]{2,1,0:T(8,128)(2,1)}, u32[]{:S(2)}) copy-start(bf16[3,2048,256]{2,1,0:T(8,128)(2,1)} %param.18) | copy-start | bytes 9437188
  6.5 107.7 %all-reduce.2.cloned.1.call-start = ((), (), s32[]{:S(2)}) async-start(), calls=%async_computation.2 | async-start | bytes 262144 | tf_op jit(solution)/shard_map/psum | solution.py:92
  53.3 122.5 %all-gather.4.cloned.1.call-start = ((), (), s32[]{:S(2)}) async-start(), calls=%async_computation.3 | async-start | bytes 2228224 | tf_op jit(solution)/shard_map/all_gather | solution.py:15
  117.0 138.8 %reduce-scatter.3.cloned.1.call-start = ((), (), s32[]{:S(2)}) async-start(), calls=%async_computation.4 | async-start | bytes 2228224 | tf_op jit(solution)/shard_map/reduce_scatter | solution.py:123
  122.3 6.5 %copy-start.1 = (f32[32,8]{0,1:T(8,128)S(1)}, f32[32,8]{0,1:T(8,128)}, u32[]{:S(2)}) copy-start(f32[32,8]{0,1:T(8,128)} %param.17) | copy-start | bytes 3076
  181.0 1.6 copy-start.2
  185.2 102.3 %reduce-scatter.5.cloned.1.call-start = ((), (), s32[]{:S(2)}) async-start(), calls=%async_computation.5 | async-start | bytes 147456 | tf_op jit(solution)/shard_map/reduce_scatter | solution.py:129
Sparse Core Ops, SparseCore 0:
  53.4 60.8 all-reduce.1
  117.1 44.3 all-gather.3
  185.4 70.3 reduce-scatter.2
  258.0 29.4 reduce-scatter.4
where the time goes:
time: 296 us; the launch traced here: 295 us
  waiting for transfers between devices  163 us (55%)
  blocking collectives  60.2 us (20%)
  local copies, waits for them, and re-layouts  33.1 us (11%)
  matrix products  16.1 us (5%)
  between operations  14 us (5%)
  other arithmetic  8.33 us (3%)
    reduce_scatter x1, waiting for transfers between devices, per_device(): lax.psum_scatter(jnp.dot(gathered, w_down_flat, preferred_element_type=jn...  70.5 us
    psum x1, waiting for transfers between devices, per_device(): lax.psum(head_terms.astype(jnp.bfloat16), 'head').astype(jnp.float32)  60.9 us
    all_gather x2, blocking collectives, over_all(): return work(lax.all_gather(shard, axis, axis=dim, tiled=True), jnp.int32(0))  46.6 us
    reduce_scatter x1, waiting for transfers between devices, per_device(): lax.psum_scatter(token_sums, 'head', scatter_dimension=1, tiled=True)  31.7 us
    all_gather x1, blocking collectives, per_device(): full_rows = lax.all_gather(hidden, 'head', axis=1, tiled=True)  13.6 us
    dynamic_slice x3, local copies, waits for them, and re-layouts, score_block(): lax.dynamic_slice_in_dim(k_cache, block_idx * KEY_BLOCK, KEY_BLOCK, 1)  9.85 us
    dynamic_slice x3, local copies, waits for them, and re-layouts, value_block(): lax.dynamic_slice_in_dim(v_cache, block_idx * KEY_BLOCK, KEY_BLOCK, 1)  9.85 us
    unnamed x8, local copies, waits for them, and re-layouts  6.58 us
  transfers between devices with their start and end apart: 4, of which 3 were waited for; matrix products, arithmetic and copies ran while one was open for 4% of the time, Pallas kernels for 0%

commit v1 on v0

v1 whole, which is shorter than its diff:
```python
import functools

import jax
import jax.numpy as jnp
import numpy as np
from jax import lax
from jax.experimental import pallas as pl
from jax.experimental.pallas import tpu as pltpu
from jax.sharding import PartitionSpec as P

MESH = pl.DeviceIdType.MESH
BF = jnp.bfloat16
F32 = jnp.float32

D = 2048
ROWS = 32
TOKENS = 512
HD = 128
LEN = 384
COLS = 2 * LEN
rope_theta = 50000.0
norm_eps = 1e-05
SCALE = HD ** (-0.5)


def dot(a, b):
    return jnp.dot(a, b, preferred_element_type=F32)


def kernel(
    hidden_ref, len_ref, cos_ref, sin_ref, share_ref,
    wqkv_hbm, wout_hbm, k_hbm, v_hbm, win_hbm, wdown_hbm,
    out_ref,
    wqkv, wout, kbuf, vbuf, wraw, wrel, wdown,
    hid, qs, sc, att, cts, ctr, resid, gath, tshare, acc, ssq, units,
    psend, xrecv, ssum, ea_r, ea_f, eb_r, eb_f, a1, b1, ea2_r, ea2_f, eb2_r, eb2_f, csum, yrecv,
    ld_sem, hs_sem, hr_sem, cs_sem, cr_sem, ds_sem, dr_sem, ag_s, ag_r, dd_s, dd_r,
    ps_s, ps_r, rs_s, rs_r, ys_s, ys_r,
):
    me_r = lax.axis_index("req")
    me_h = lax.axis_index("head")
    x, z = me_r // 4, me_r % 4
    y, c = me_h // 2, me_h % 2
    xp, xm, x2 = (x + 1) % 4, (x + 3) % 4, (x + 2) % 4
    zp, zm, z2 = (z + 1) % 4, (z + 3) % 4, (z + 2) % 4
    dev_xp, dev_xm = (xp * 4 + z, me_h), (xm * 4 + z, me_h)
    dev_zp, dev_zm = (x * 4 + zp, me_h), (x * 4 + zm, me_h)
    other = (me_r, y * 2 + (1 - c))

    loads = []

    def load(src, dst):
        copy = pltpu.make_async_copy(src, dst, ld_sem.at[len(loads)])
        copy.start()
        loads.append(copy)
        return copy

    ld_wqkv = load(wqkv_hbm, wqkv)
    ld_win = load(win_hbm, wraw)
    ld_k = [load(k_hbm.at[pl.ds(8 * g, 8)], kbuf.at[pl.ds(8 * g, 8)]) for g in range(4)]
    ld_v = [load(v_hbm.at[pl.ds(8 * g, 8)], vbuf.at[pl.ds(8 * g, 8)]) for g in range(4)]
    ld_wout = [load(wout_hbm.at[:, pl.ds(256 * j, 256)], wout.at[j]) for j in range(8)]
    ld_wdown = [load(wdown_hbm.at[:, pl.ds(256 * j, 256)], wdown.at[j]) for j in range(8)]

    barrier = pltpu.get_barrier_semaphore()
    for k in range(1, 8):
        pl.semaphore_signal(
            barrier, inc=1, device_id=(me_r, (me_h + k) % 8), device_id_type=MESH
        )
    for dev in (dev_xp, dev_xm, dev_zp, dev_zm):
        pl.semaphore_signal(barrier, inc=1, device_id=dev, device_id_type=MESH)
    pl.semaphore_wait(barrier, 11)

    sends = []

    def push(src, dst, s_sem, r_sem, dev):
        copy = pltpu.make_async_remote_copy(
            src_ref=src, dst_ref=dst, send_sem=s_sem, recv_sem=r_sem,
            device_id=dev, device_id_type=MESH,
        )
        copy.start()
        sends.append(copy)
        return copy

    order = (4, 5, 3, 2, 6, 7, 1)
    got_hid = {
        k: push(
            hidden_ref, hid.at[me_h], hs_sem.at[k - 1], hr_sem.at[k - 1],
            (me_r, (me_h + k) % 8),
        )
        for k in order
    }

    class Ring:
        def __init__(self, idx, full, halves, me, plus, minus, dev_p, dev_m):
            self.idx, self.full, self.halves = idx, full, halves
            self.plus, self.minus, self.dev_p, self.dev_m, self.me = plus, minus, dev_p, dev_m, me

        def _push(self, ref, n, dev):
            return push(ref, ref, ag_s.at[self.idx, n], ag_r.at[self.idx, n], dev)

        def start(self):
            own = self.full(self.me)
            self.from_m = self._push(own, 0, self.dev_p)
            self.from_p = self._push(own, 1, self.dev_m)

        def relay_m(self):
            self.from_m.wait_recv()
            self.half0 = self._push(self.halves(self.minus)[0], 2, self.dev_p)

        def relay_p(self):
            self.from_p.wait_recv()
            self.half1 = self._push(self.halves(self.plus)[1], 3, self.dev_m)

        def finish0(self):
            self.half0.wait_recv()

        def finish1(self):
            self.half1.wait_recv()

    def along_x(idx, full, halves):
        return Ring(idx, full, halves, x, xp, xm, dev_xp, dev_xm)

    def along_z(idx, full, halves):
        return Ring(idx, full, halves, z, zp, zm, dev_zp, dev_zm)

    t1 = along_z(
        0,
        lambda a: tshare.at[x, a],
        lambda a: (tshare.at[x, a, pl.ds(0, 16)], tshare.at[x, a, pl.ds(16, 16)]),
    )
    t2 = along_x(
        1,
        lambda a: tshare.at[a],
        lambda a: (tshare.at[a, pl.ds(0, 2)], tshare.at[a, pl.ds(2, 2)]),
    )
    ring_a1 = along_z(
        2,
        lambda a: gath.at[pl.ds(0, 2), c, x, a],
        lambda a: (gath.at[0, c, x, a], gath.at[1, c, x, a]),
    )
    ring_b1 = along_x(
        3,
        lambda a: gath.at[pl.ds(2, 2), c, a, z],
        lambda a: (gath.at[2, c, a, z], gath.at[3, c, a, z]),
    )
    ring_a2 = along_x(
        4,
        lambda a: gath.at[pl.ds(0, 2), c, a],
        lambda a: (gath.at[0, c, a], gath.at[1, c, a]),
    )
    ring_b2 = along_z(
        5,
        lambda a: gath.at[pl.ds(2, 2), c, :, a],
        lambda a: (gath.at[2, c, :, a], gath.at[3, c, :, a]),
    )

    tshare[x, z] = share_ref[...]
    t1.start()

    ld_win.wait()
    row_i = lax.broadcasted_iota(jnp.int32, (256, 256), 0)
    col_i = lax.broadcasted_iota(jnp.int32, (256, 256), 1)
    perm = jnp.where(
        ((row_i & 31) == (col_i >> 3)) & ((row_i >> 5) == (col_i & 7)), 1.0, 0.0
    ).astype(BF)

    def relay_out(lo, hi):
        def body(it, carry):
            base = pl.multiple_of(it * 512, 512)
            out_base = pl.multiple_of(it * 64, 64)
            rhs = jnp.concatenate(
                [wraw[pl.ds(base, 256), :], wraw[pl.ds(base + 256, 256), :]], axis=1
            )
            res = dot(perm, rhs).astype(BF)
            for e in range(8):
                for s in range(2):
                    wrel[pl.ds(out_base + 32 * s, 32), 128 * e : 128 * (e + 1)] = res[
                        32 * e : 32 * (e + 1), 128 * s : 128 * (s + 1)
                    ]
            return carry

        lax.fori_loop(lo, hi, body, 0)

    relay_out(0, 16)

    ld_wqkv.wait()

    def project(block, slot):
        xf = block.astype(F32)
        return [dot(block, wqkv[i, slot]) for i in range(3)], jnp.sum(
            xf * xf, axis=-1, keepdims=True
        )

    proj, squares = project(hidden_ref[...], me_h)
    for k in (1, 7, 6, 2, 3, 5, 4):
        got_hid[k].wait_recv()
        slot = (me_h + 8 - k) % 8
        more, sq = project(hid[slot], slot)
        proj = [a + b for a, b in zip(proj, more)]
        squares = squares + sq
    rs = lax.rsqrt(squares * (1.0 / D) + norm_eps)
    cosine, sine = cos_ref[...], sin_ref[...]
    q_f, k_f, v_f = [], [], []
    for h in range(2):
        part = [p[:, HD * h : HD * (h + 1)] * rs for p in proj]

        def turned(v):
            swapped = jnp.concatenate([v[:, HD // 2 :], v[:, : HD // 2]], axis=1)
            return (v * cosine + swapped * sine).astype(BF).astype(F32)

        q_f.append(turned(part[0]))
        k_f.append(turned(part[1]))
        v_f.append(part[2].astype(BF).astype(F32))
        qs[h] = q_f[h]

    t1.relay_m()
    t1.relay_p()

    for copy in ld_k:
        copy.wait()
    owner16 = lax.broadcasted_iota(jnp.int32, (16, COLS), 0) & 7
    owner16s = lax.broadcasted_iota(jnp.int32, (16, HD), 0) & 7

    def score_group(g, carry):
        base = pl.multiple_of(g * 8, 8)
        query = qs[:, pl.ds(base, 8), :].reshape(16, HD).astype(BF)
        out = None
        for i in range(8):
            s = lax.dot_general(
                query, kbuf[g * 8 + i], (((1,), (1,)), ((), ())), preferred_element_type=F32
            )
            out = s if i == 0 else jnp.where(owner16 == i, s, out)
        sc[:, pl.ds(base, 8), :] = out.reshape(2, 8, COLS)
        return carry

    lax.fori_loop(0, 4, score_group, 0)

    t1.finish0()
    t1.finish1()
    t2.start()

    position = lax.broadcasted_iota(jnp.int32, (ROWS, COLS), 1)
    limit = len_ref[...] * 2
    self_w = []
    for h in range(2):
        valid = ((position & 1) == h) & (position < limit)
        s = jnp.where(valid, sc[h] * SCALE, -jnp.inf)
        self_score = jnp.sum(q_f[h] * k_f[h], axis=-1, keepdims=True) * SCALE
        top = jnp.maximum(jnp.max(s, axis=-1, keepdims=True), self_score)
        e = jnp.exp(s - top)
        self_e = jnp.exp(self_score - top)
        inv = 1.0 / (jnp.sum(e, axis=-1, keepdims=True) + self_e)
        sc[h] = e * inv
        self_w.append((self_e * inv).astype(BF).astype(F32))

    for copy in ld_v:
        copy.wait()

    def value_group(g, carry):
        base = pl.multiple_of(g * 8, 8)
        weights = sc[:, pl.ds(base, 8), :].reshape(16, COLS).astype(BF)
        out = None
        for i in range(8):
            s = dot(weights, vbuf[g * 8 + i])
            out = s if i == 0 else jnp.where(owner16s == i, s, out)
        att[:, pl.ds(base, 8), :] = out.reshape(2, 8, HD)
        return carry

    lax.fori_loop(0, 4, value_group, 0)
    attended = jnp.concatenate(
        [(att[h] + self_w[h] * v_f[h]).astype(BF) for h in range(2)], axis=1
    )

    for copy in ld_wout:
        copy.wait()
    for j in range(8):
        cts[j] = dot(attended, wout[j]).astype(BF)
    got_c = {
        k: push(
            cts.at[(me_h + k) % 8], ctr.at[me_h], cs_sem.at[k - 1], cr_sem.at[k - 1],
            (me_r, (me_h + k) % 8),
        )
        for k in order
    }
    t2.relay_m()
    t2.relay_p()
    relay_out(16, 32)
    total = hidden_ref[...].astype(F32) + cts[me_h].astype(F32)
    for k in (1, 7, 6, 2, 3, 5, 4):
        got_c[k].wait_recv()
        total = total + ctr[(me_h + 8 - k) % 8].astype(F32)
    resid[...] = total
    gath[y, c, x, z] = total.astype(BF)

    got_d = [
        push(
            gath.at[y, c, x, z], gath.at[y, c, x, z], ds_sem.at[k - 1], dr_sem.at[k - 1],
            (me_r, ((y + k) % 4) * 2 + c),
        )
        for k in (2, 1, 3)
    ]
    for copy in got_d:
        copy.wait_recv()

    pieces = []

    def hand(ref):
        n = len(pieces)
        pieces.append(push(ref, ref, dd_s.at[n], dd_r.at[n], other))
        return pieces[-1]

    ring_a1.start()
    ring_b1.start()
    ring_a1.relay_m()
    ring_b1.relay_m()
    ring_a1.relay_p()
    ring_b1.relay_p()
    ring_a1.finish0()
    ring_a1.finish1()
    ring_a2.start()
    a_own = hand(gath.at[pl.ds(0, 2), c, x])
    ring_b1.finish0()
    ring_b1.finish1()
    ring_b2.start()
    b_own = hand(gath.at[pl.ds(2, 2), c, :, z])

    def squares_of(rows):
        f = rows.astype(F32)
        f = f * f
        out = f[:, :128]
        for i in range(1, 8):
            out = out + f[:, 128 * i : 128 * (i + 1)]
        return out

    def gate_up(rows, first, store):
        def body(n, carry):
            cols = pl.ds(pl.multiple_of(n * 256, 256), 256)
            store(cols, dot(rows, wrel[first : first + 1024, cols]))
            return carry

        lax.fori_loop(0, 4, body, 0)

    def part_a(xx):
        rows = jnp.concatenate(
            [gath[yy, cc, xx].reshape(128, 256) for yy in (0, 1) for cc in (0, 1)], axis=1
        )
        ssq[xx] = squares_of(rows).reshape(4, ROWS, 128)

        def store(cols, val):
            acc[xx, :, :, cols] = val.reshape(4, ROWS, 256)

        gate_up(rows, 0, store)

    def part_b(zz):
        rows = jnp.concatenate(
            [gath[yy, cc, :, zz].reshape(128, 256) for yy in (2, 3) for cc in (0, 1)], axis=1
        )
        ssq[:, zz] += squares_of(rows).reshape(4, ROWS, 128)

        def store(cols, val):
            acc[:, zz, :, cols] += val.reshape(4, ROWS, 256)

        gate_up(rows, 1024, store)

    a_own.wait_recv()
    part_a(x)
    ring_a2.relay_m()
    a_m = hand(gath.at[pl.ds(0, 2), c, xm])
    ring_b2.relay_m()
    b_m = hand(gath.at[pl.ds(2, 2), c, :, zm])
    ring_a2.relay_p()
    a_p = hand(gath.at[pl.ds(0, 2), c, xp])
    ring_b2.relay_p()
    b_p = hand(gath.at[pl.ds(2, 2), c, :, zp])
    a_m.wait_recv()
    part_a(xm)
    a_p.wait_recv()
    part_a(xp)
    ring_a2.finish0()
    a_20 = hand(gath.at[0, c, x2])
    ring_a2.finish1()
    a_21 = hand(gath.at[1, c, x2])
    ring_b2.finish0()
    b_20 = hand(gath.at[2, c, :, z2])
    ring_b2.finish1()
    b_21 = hand(gath.at[3, c, :, z2])
    t2.finish0()
    t2.finish1()
    a_20.wait_recv()
    a_21.wait_recv()
    part_a(x2)
    b_own.wait_recv()
    part_b(z)
    b_m.wait_recv()
    part_b(zm)
    b_p.wait_recv()
    part_b(zp)
    b_20.wait_recv()
    b_21.wait_recv()
    part_b(z2)

    e_row = lax.broadcasted_iota(jnp.int32, (128, HD), 0)
    e_lane = lax.broadcasted_iota(jnp.int32, (128, HD), 1)
    low = lax.broadcasted_iota(jnp.int32, (128, HD), 1) < 64

    def unit_rows(xx, carry):
        mean = jnp.sum(ssq[xx].reshape(128, 128), axis=-1, keepdims=True) * (1.0 / D)
        scale = lax.rsqrt(mean + norm_eps)
        shares = tshare[xx].reshape(128, 128)
        for p in range(4):
            pick = jnp.where(
                (e_row < 16) & ((e_row & 7) == 2 * p + (e_lane >> 6)), 1.0, 0.0
            ).astype(BF)
            share = dot(shares, pick)
            even = acc[xx, :, :, 256 * p : 256 * p + 128].reshape(128, 128) * scale
            odd = acc[xx, :, :, 256 * p + 128 : 256 * p + 256].reshape(128, 128) * scale
            gate = jnp.where(low, even, pltpu.roll(odd, 64, 1))
            upward = jnp.where(low, pltpu.roll(even, 64, 1), odd)
            silu = gate / (1.0 + jnp.exp(-gate))
            units[xx, :, :, 128 * p : 128 * (p + 1)] = (
                (share * (silu * upward)).astype(BF).reshape(4, ROWS, 128)
            )
        return carry

    lax.fori_loop(0, 4, unit_rows, 0)

    for copy in ld_wdown:
        copy.wait()
    got_x = []
    for yy in range(4):
        def give(xx, carry, yy=yy):
            val = dot(units[xx].reshape(128, 512), wdown[yy * 2 + (1 - c)])
            psend[yy, xx] = val.astype(BF).reshape(4, ROWS, 256)
            return carry

        lax.fori_loop(0, 4, give, 0)
        got_x.append(push(psend.at[yy], xrecv.at[yy], ps_s.at[yy], ps_r.at[yy], other))

    def keep_block(yy):
        got_x[yy].wait_recv()

        def body(xx, carry):
            val = dot(units[xx].reshape(128, 512), wdown[yy * 2 + c])
            val = val + xrecv[yy, xx].reshape(128, 256).astype(F32)
            ssum[yy, xx] = val.astype(BF).reshape(4, ROWS, 256)
            return carry

        lax.fori_loop(0, 4, body, 0)

    class Reduce:
        def __init__(self, idx, ref, blk, relay, final, me, plus, minus, opp, dev_p, dev_m):
            self.idx, self.ref, self.blk, self.relay, self.final = idx, ref, blk, relay, final
            self.me, self.plus, self.minus, self.opp = me, plus, minus, opp
            self.dev_p, self.dev_m = dev_p, dev_m

        def _push(self, src, dst, n, dev):
            return push(src, dst, rs_s.at[self.idx, n], rs_r.at[self.idx, n], dev)

        def start(self):
            at = lambda hf, a: self.ref.at[self.blk(hf, a)]
            self.r0 = self._push(at(0, self.opp), self.relay.at[0], 0, self.dev_p)
            self.r1 = self._push(at(1, self.opp), self.relay.at[1], 1, self.dev_m)
            self.p1 = self._push(at(1, self.plus), self.final.at[0, 1], 2, self.dev_p)
            self.m0 = self._push(at(0, self.minus), self.final.at[1, 0], 3, self.dev_m)

        def _add(self, hf, a, got):
            i = self.blk(hf, a)
            self.ref[i] = (self.ref[i].astype(F32) + got.astype(F32)).astype(BF)

        def relay0(self):
            self.r0.wait_recv()
            self._add(0, self.plus, self.relay[0])
            self.p0 = self._push(
                self.ref.at[self.blk(0, self.plus)], self.final.at[0, 0], 4, self.dev_p
            )

        def relay1(self):
            self.r1.wait_recv()
            self._add(1, self.minus, self.relay[1])
            self.m1 = self._push(
                self.ref.at[self.blk(1, self.minus)], self.final.at[1, 1], 5, self.dev_m
            )

        def wait(self):
            for copy in (self.p1, self.m0, self.p0, self.m1):
                copy.wait_recv()

        def own(self, hf):
            return (
                self.ref[self.blk(hf, self.me)].astype(F32)
                + self.final[0, hf].astype(F32)
                + self.final[1, hf].astype(F32)
            )

    def reduce_x(idx, ref, blk, relay, final):
        return Reduce(idx, ref, blk, relay, final, x, xp, xm, x2, dev_xp, dev_xm)

    def reduce_z(idx, ref, blk, relay, final):
        return Reduce(idx, ref, blk, relay, final, z, zp, zm, z2, dev_zp, dev_zm)

    all4 = slice(None)
    ea1 = reduce_x(0, ssum, lambda hf, a: (hf, a), ea_r, ea_f)
    eb1 = reduce_z(1, ssum, lambda hf, a: (2 + hf, all4, a), eb_r, eb_f)
    ea2 = reduce_z(2, a1, lambda hf, a: (hf, a), ea2_r, ea2_f)
    eb2 = reduce_x(3, b1, lambda hf, a: (hf, a), eb2_r, eb2_f)

    keep_block(0)
    keep_block(1)
    ea1.start()
    keep_block(2)
    keep_block(3)
    eb1.start()
    ea1.relay0()
    ea1.relay1()
    eb1.relay0()
    eb1.relay1()
    ea1.wait()
    for hf in range(2):
        a1[hf] = ea1.own(hf).astype(BF)
    ea2.start()
    eb1.wait()
    for hf in range(2):
        b1[hf] = eb1.own(hf).astype(BF)
    eb2.start()
    ea2.relay0()
    ea2.relay1()
    eb2.relay0()
    eb2.relay1()
    ea2.wait()
    for hf in range(2):
        csum[hf] = ea2.own(hf).astype(BF)
    eb2.wait()
    for hf in range(2):
        csum[2 + hf] = eb2.own(hf).astype(BF)

    got_y = [
        push(
            csum.at[(y + k) % 4], yrecv.at[k - 1], ys_s.at[k - 1], ys_r.at[k - 1],
            (me_r, ((y + k) % 4) * 2 + c),
        )
        for k in (2, 1, 3)
    ]
    result = resid[...] + csum[y].astype(F32)
    for copy in got_y:
        copy.wait_recv()
    for k in range(3):
        result = result + yrecv[k].astype(F32)
    out_ref[...] = result.astype(BF)
    for copy in sends:
        copy.wait_send()


def layer(hidden, lengths, expert_ids, route_weights, w_qkv, w_out, k_cache, v_cache, w_in, w_down):
    half = HD // 2
    freqs = jnp.asarray(
        np.tile(rope_theta ** (-np.arange(half, dtype=np.float64) / half), 2).astype(np.float32)
    )
    sign = jnp.asarray(np.repeat([-1.0, 1.0], half).astype(np.float32))
    angles = lengths.astype(F32)[:, None] * freqs[None, :]
    cosine, sine = jnp.cos(angles), jnp.sin(angles) * sign[None, :]
    lane = jnp.arange(128, dtype=jnp.int32)
    wanted = lax.axis_index("head") * 8 + (lane & 7)
    share = jnp.sum(
        route_weights[:, :, None] * (expert_ids[:, :, None] == wanted[None, None, :]).astype(F32),
        axis=1,
    )
    high = share.astype(BF)
    lower = (share - high.astype(F32)).astype(BF)
    share = jnp.where(lane < 8, high, jnp.where(lane < 16, lower, jnp.zeros_like(high)))

    vm = pl.BlockSpec(memory_space=pltpu.VMEM)
    hbm = pl.BlockSpec(memory_space=pl.ANY)
    V = pltpu.VMEM
    dma = pltpu.SemaphoreType.DMA
    return pl.pallas_call(
        kernel,
        out_shape=jax.ShapeDtypeStruct((ROWS, 256), BF),
        in_specs=[vm] * 5 + [hbm] * 6,
        out_specs=vm,
        scratch_shapes=[
            V((3, 8, 256, 256), BF), V((8, 256, 256), BF), V((ROWS, COLS, HD), BF),
            V((ROWS, COLS, HD), BF), V((16384, 128), BF), V((2048, 1024), BF), V((8, 512, 256), BF),
            V((8, ROWS, 256), BF), V((2, ROWS, HD), F32), V((2, ROWS, COLS), F32),
            V((2, ROWS, HD), F32), V((8, ROWS, 256), BF), V((8, ROWS, 256), BF),
            V((ROWS, 256), F32), V((4, 2, 4, 4, ROWS, 256), BF), V((4, 4, ROWS, 128), BF),
            V((4, 4, ROWS, 1024), F32), V((4, 4, ROWS, 128), F32), V((4, 4, ROWS, 512), BF),
            V((4, 4, 4, ROWS, 256), BF), V((4, 4, 4, ROWS, 256), BF), V((4, 4, 4, ROWS, 256), BF),
            V((2, 4, ROWS, 256), BF), V((2, 2, 4, ROWS, 256), BF),
            V((2, 4, ROWS, 256), BF), V((2, 2, 4, ROWS, 256), BF),
            V((2, 4, ROWS, 256), BF), V((2, 4, ROWS, 256), BF),
            V((2, ROWS, 256), BF), V((2, 2, ROWS, 256), BF),
            V((2, ROWS, 256), BF), V((2, 2, ROWS, 256), BF),
            V((4, ROWS, 256), BF), V((3, ROWS, 256), BF),
            dma((26,)), dma((7,)), dma((7,)), dma((7,)), dma((7,)), dma((3,)), dma((3,)),
            dma((6, 4)), dma((6, 4)), dma((10,)), dma((10,)),
            dma((4,)), dma((4,)), dma((4, 6)), dma((4, 6)), dma((3,)), dma((3,)),
        ],
        compiler_params=pltpu.CompilerParams(
            collective_id=0, has_side_effects=True, vmem_limit_bytes=60 * 1024 * 1024
        ),
    )(
        hidden, lengths[:, None], cosine, sine, share,
        w_qkv.reshape(3, 8, 256, 256), w_out,
        k_cache.reshape(ROWS, COLS, HD), v_cache.reshape(ROWS, COLS, HD),
        w_in.reshape(16384, 128), w_down.reshape(512, D),
    )


def solution(mesh):
    in_specs = (
        P("req", "head"),
        P("req"),
        P("req", None),
        P("req", None),
        P(None, None, "head"),
        P("head", None),
        P("req", None, "head", None),
        P("req", None, "head", None),
        P(None, "head", "req"),
        P("head", "req", None),
    )
    return jax.shard_map(
        layer, mesh=mesh, in_specs=in_specs, out_specs=P("req", "head"), check_vma=False
    )
```

time: 296 us -> 81.7 us (0.28)
  waiting for transfers between devices: 163 us -> 0 us
  Pallas kernels: 0 us -> 74.3 us
  blocking collectives: 60.2 us -> 0 us
  local copies, waits for them, and re-layouts: 33.1 us -> 4.19 us
  matrix products: 16.1 us -> 0 us
  between operations: 14 us -> 0.02 us
  other arithmetic: 8.33 us -> 2.82 us
    reduce_scatter x2 -> x0, waiting for transfers between devices: 102 us -> none  [the longest x1 70.5 us: per_device(): lax.psum_scatter(jnp.dot(gathered, w_down_flat, preferred_element_type=jn...]
    pallas_call x0 -> x1, Pallas kernels: none -> 74.3 us  [layer(): pl.pallas_call(kernel, out_shape=jax.ShapeDtypeStruct((ROWS, 256), BF), i...]
    psum x1 -> x0, waiting for transfers between devices: 60.9 us -> none  [per_device(): lax.psum(head_terms.astype(jnp.bfloat16), 'head').astype(jnp.float32)]
    all_gather x3 -> x0, blocking collectives: 60.2 us -> none  [the longest x2 46.6 us: over_all(): return work(lax.all_gather(shard, axis, axis=dim, tiled=True), jnp.int32(0))]
    dynamic_slice x9 -> x0, local copies, waits for them, and re-layouts: 19.8 us -> none  [the longest x3 9.85 us: score_block(): lax.dynamic_slice_in_dim(k_cache, block_idx * KEY_BLOCK, KEY_BLOCK, 1)]
    dot_general x10 -> x0, matrix products: 16.1 us -> none  [the longest x1 5.19 us: expert_hidden(): gate_up = jnp.dot(token_rows, w_in_flat, preferred_element_type=jnp.float32)]
    dot_general x1 -> x0, local copies, waits for them, and re-layouts: 6.51 us -> none  [expert_hidden(): gate_up = jnp.dot(token_rows, w_in_flat, preferred_element_type=jnp.float32)]
    convert_element_type x8 -> x1, other arithmetic: 5.15 us -> 0.66 us  [layer(): angles = lengths.astype(F32)[:, None] * freqs[None, :]]
  transfers between devices with their start and end apart: 4 -> 0, of which waited for: 3 -> 0; matrix products, arithmetic and copies ran while one was open for 4% -> 0% of each run, Pallas kernels for 0% -> 0%
where the time goes in v1:
time: 81.7 us; the launch traced here: 81.3 us
  Pallas kernels  74.3 us (91%)
  local copies, waits for them, and re-layouts  4.19 us (5%)
  other arithmetic  2.82 us (3%)
    pallas_call x1, Pallas kernels, layer(): pl.pallas_call(kernel, out_shape=jax.ShapeDtypeStruct((ROWS, 256), BF), i...  74.3 us
    unnamed x3, local copies, waits for them, and re-layouts  2.85 us

profile of v1, /device:TPU:0, one launch (start us, length us, event | category | flops | bytes accessed | tf_op | source)
XLA Modules:
  0.0 81.3 jit_solution(7354162580380548461)
XLA Ops:
  0.0 0.7 convert_element_type.13
  0.7 0.8 copy.16
  1.4 0.8 copy.17
  2.2 0.1 select_reduce_fusion
  2.3 0.6 fusion.2.share_ref
  2.9 1.3 %copy.18.len_ref = s32[32,1]{1,0:T(8,128)} copy(s32[32,1]{0,1:T(1,128)} %bitcast.11) | data formatting | bytes 256 | tf_op jit(solution)/shard_map/broadcast_in_dim | solution.py:603
  4.3 1.4 %fusion = (f32[32,128]{1,0:T(8,128)}, f32[32,128]{1,0:T(8,128)}) fusion(f32[128]{0:T(128)} %constant.21.clone, f32[128]{0:T(128)} %constant.20.clone, f32[32]{0:T(128)S(1)} %convert_element_type.13), kind=kLoop, calls=%fused_computation.3 | loop fusion | flops 8192 | bytes 33920 | tf_op jit(solution)/shard_map/mul | solution.py:561
  5.7 74.3 %shard_map.118 = bf16[32,256]{1,0:T(8,128)(2,1)} custom-call(bf16[32,256]{1,0:T(8,128)(2,1)} %hidden_ref.1, s32[32,1]{1,0:T(8,128)} %copy.18.len_ref, f32[32,128]{1,0:T(8,128)} %get-tuple-element.6.cos_ref, f32[32,128]{1,0:T(8,128)} %get-tuple-element.5.sin_ref, bf16[32,128]{1,0:T(8,128)(2,1)} %fusion.2.share_ref, bf16[3,8,256,256]{3,2,1,0:T(8,128)(2,1)} %bitcast.9, ...), custom_call_target="tpu_custom_call" | custom-call | tf_op jit(solution)/shard_map/pallas_call | solution.py:576
  80.0 1.3 %copy.20 = bf16[32,256]{1,0:T(8,128)(2,1)} copy(bf16[32,256]{1,0:T(8,128)(2,1)} %shard_map.118) | data formatting | bytes 32768
  (2 shorter events, 0.0 us)

commit v2 on v0

v2 whole, which is shorter than its diff:
```python
import functools

import jax
import jax.numpy as jnp
import numpy as np
from jax import lax
from jax.experimental import pallas as pl
from jax.experimental.pallas import tpu as pltpu
from jax.sharding import PartitionSpec as P

MESH = pl.DeviceIdType.MESH
BF = jnp.bfloat16
F32 = jnp.float32

D = 2048
ROWS = 32
TOKENS = 512
HD = 128
LEN = 384
COLS = 2 * LEN
rope_theta = 50000.0
norm_eps = 1e-05
SCALE = HD ** (-0.5)


def dot(a, b):
    return jnp.dot(a, b, preferred_element_type=F32)


def kernel(
    freq_ref, sign_ref, hidden_ref, len_ref, ids_ref, rw_ref,
    wqkv_hbm, wout_hbm, k_hbm, v_hbm, win_hbm, wdown_hbm,
    out_ref,
    wqkv, wout, kbuf, vbuf, wraw, wrel, wdown,
    hid, qs, sc, att, cts, ctr, resid, gath, tshare, xs, units, psend, xrecv, ssum, yrecv,
    ld_sem, hs_sem, hr_sem, cs_sem, cr_sem, t_s, t_r, d_s, d_r, dd_s, dd_r,
    ps_s, ps_r, e_s, e_r, plane_sem, cube_sem,
):
    me_r = lax.axis_index("req")
    me_h = lax.axis_index("head")
    x, z = me_r // 4, me_r % 4
    y, c = me_h // 2, me_h % 2
    other = (me_r, y * 2 + (1 - c))

    def at(dx, dy, dz):
        return ((x + dx) % 4) * 4 + (z + dz) % 4, ((y + dy) % 4) * 2 + c

    loads = []

    def load(src, dst):
        copy = pltpu.make_async_copy(src, dst, ld_sem.at[len(loads)])
        copy.start()
        loads.append(copy)
        return copy

    ld_wqkv = load(wqkv_hbm, wqkv)
    ld_k = [load(k_hbm.at[pl.ds(8 * g, 8)], kbuf.at[pl.ds(8 * g, 8)]) for g in range(4)]
    ld_v = [load(v_hbm.at[pl.ds(8 * g, 8)], vbuf.at[pl.ds(8 * g, 8)]) for g in range(4)]
    ld_wout = [load(wout_hbm.at[:, pl.ds(256 * j, 256)], wout.at[j]) for j in range(8)]
    ld_win = load(win_hbm, wraw)
    ld_wdown = [load(wdown_hbm.at[:, pl.ds(256 * j, 256)], wdown.at[j]) for j in range(8)]

    barrier = pltpu.get_barrier_semaphore()

    def tell(sem, dev):
        pl.semaphore_signal(sem, inc=1, device_id=dev, device_id_type=MESH)

    for k in range(1, 8):
        tell(barrier, (me_r, (me_h + k) % 8))
    for k in range(1, 4):
        tell(barrier, at(k, 0, 0))
        tell(barrier, at(0, 0, k))

    expert = lax.broadcasted_iota(jnp.int32, (8, ROWS), 0) + me_h * 8
    share = jnp.zeros((8, ROWS), F32)
    for k in range(8):
        share = share + jnp.where(ids_ref[k : k + 1, :] == expert, rw_ref[k : k + 1, :], 0.0)
    high = share.astype(BF)
    lower = (share - high.astype(F32)).astype(BF)
    both = jnp.concatenate([high.astype(F32), lower.astype(F32)], axis=0).astype(BF)
    eye = jnp.where(
        lax.broadcasted_iota(jnp.int32, (16, 128), 0)
        == lax.broadcasted_iota(jnp.int32, (16, 128), 1),
        1.0,
        0.0,
    ).astype(BF)
    tshare[z, x] = lax.dot_general(
        both, eye, (((0,), (0,)), ((), ())), preferred_element_type=F32
    ).astype(BF)
    length = jnp.sum(
        jnp.where(
            lax.broadcasted_iota(jnp.int32, (ROWS, ROWS), 0)
            == lax.broadcasted_iota(jnp.int32, (ROWS, ROWS), 1),
            len_ref[...].astype(F32),
            0.0,
        ),
        axis=1,
        keepdims=True,
    )
    angles = length * freq_ref[...]
    cosine, sine = jnp.cos(angles), jnp.sin(angles) * sign_ref[...]
    limit = length.astype(jnp.int32) * 2

    pl.semaphore_wait(barrier, 13)

    def remote(src, dst, s_sem, r_sem, dev):
        return pltpu.make_async_remote_copy(
            src_ref=src, dst_ref=dst, send_sem=s_sem, recv_sem=r_sem,
            device_id=dev, device_id_type=MESH,
        )

    sends = []

    def push(src, dst, s_sem, r_sem, dev):
        copy = remote(src, dst, s_sem, r_sem, dev)
        copy.start()
        sends.append(copy)
        return copy

    order = (4, 5, 3, 2, 6, 7, 1)
    got_hid = {
        k: push(
            hidden_ref, hid.at[me_h], hs_sem.at[k - 1], hr_sem.at[k - 1],
            (me_r, (me_h + k) % 8),
        )
        for k in order
    }
    for k in range(1, 4):
        tell(plane_sem, at(0, 0, k))

    row_i = lax.broadcasted_iota(jnp.int32, (256, 256), 0)
    col_i = lax.broadcasted_iota(jnp.int32, (256, 256), 1)
    perm = jnp.where(
        ((row_i & 31) == (col_i >> 3)) & ((row_i >> 5) == (col_i & 7)), 1.0, 0.0
    ).astype(BF)

    def relay_out(lo, hi):
        def body(it, carry):
            base = pl.multiple_of(it * 512, 512)
            out_base = pl.multiple_of(it * 64, 64)
            rhs = jnp.concatenate(
                [wraw[pl.ds(base, 256), :], wraw[pl.ds(base + 256, 256), :]], axis=1
            )
            res = dot(perm, rhs).astype(BF)
            for e in range(8):
                for s in range(2):
                    wrel[pl.ds(out_base + 32 * s, 32), 128 * e : 128 * (e + 1)] = res[
                        32 * e : 32 * (e + 1), 128 * s : 128 * (s + 1)
                    ]
            return carry

        lax.fori_loop(lo, hi, body, 0)

    ld_wqkv.wait()

    def project(block, slot):
        xf = block.astype(F32)
        return [dot(block, wqkv[i, slot]) for i in range(3)], jnp.sum(
            xf * xf, axis=-1, keepdims=True
        )

    proj, squares = project(hidden_ref[...], me_h)
    for k in (1, 7, 6, 2, 3, 5, 4):
        got_hid[k].wait_recv()
        slot = (me_h + 8 - k) % 8
        more, sq = project(hid[slot], slot)
        proj = [a + b for a, b in zip(proj, more)]
        squares = squares + sq
    rs = lax.rsqrt(squares * (1.0 / D) + norm_eps)
    q_f, k_f, v_f = [], [], []
    for h in range(2):
        part = [p[:, HD * h : HD * (h + 1)] * rs for p in proj]

        def turned(v):
            swapped = jnp.concatenate([v[:, HD // 2 :], v[:, : HD // 2]], axis=1)
            return (v * cosine + swapped * sine).astype(BF).astype(F32)

        q_f.append(turned(part[0]))
        k_f.append(turned(part[1]))
        v_f.append(part[2].astype(BF).astype(F32))
        qs[h] = q_f[h]

    pl.semaphore_wait(plane_sem, 3)
    for k in range(1, 4):
        tell(cube_sem, at(0, k, 0))

    def send_share(i, carry):
        remote(tshare.at[z, x], tshare.at[z, x], t_s, t_r, at(i // 4, 0, i % 4)).start()
        return carry

    lax.fori_loop(1, 16, send_share, 0)

    for copy in ld_k:
        copy.wait()
    owner16 = lax.broadcasted_iota(jnp.int32, (16, COLS), 0) & 7
    owner16s = lax.broadcasted_iota(jnp.int32, (16, HD), 0) & 7

    def score_group(g, carry):
        base = pl.multiple_of(g * 8, 8)
        query = qs[:, pl.ds(base, 8), :].reshape(16, HD).astype(BF)
        out = None
        for i in range(8):
            s = lax.dot_general(
                query, kbuf[g * 8 + i], (((1,), (1,)), ((), ())), preferred_element_type=F32
            )
            out = s if i == 0 else jnp.where(owner16 == i, s, out)
        sc[:, pl.ds(base, 8), :] = out.reshape(2, 8, COLS)
        return carry

    lax.fori_loop(0, 4, score_group, 0)

    position = lax.broadcasted_iota(jnp.int32, (ROWS, COLS), 1)
    self_w = []
    for h in range(2):
        valid = ((position & 1) == h) & (position < limit)
        s = jnp.where(valid, sc[h] * SCALE, -jnp.inf)
        self_score = jnp.sum(q_f[h] * k_f[h], axis=-1, keepdims=True) * SCALE
        top = jnp.maximum(jnp.max(s, axis=-1, keepdims=True), self_score)
        e = jnp.exp(s - top)
        self_e = jnp.exp(self_score - top)
        inv = 1.0 / (jnp.sum(e, axis=-1, keepdims=True) + self_e)
        sc[h] = e * inv
        self_w.append((self_e * inv).astype(BF).astype(F32))

    for copy in ld_v:
        copy.wait()

    def value_group(g, carry):
        base = pl.multiple_of(g * 8, 8)
        weights = sc[:, pl.ds(base, 8), :].reshape(16, COLS).astype(BF)
        out = None
        for i in range(8):
            s = dot(weights, vbuf[g * 8 + i])
            out = s if i == 0 else jnp.where(owner16s == i, s, out)
        att[:, pl.ds(base, 8), :] = out.reshape(2, 8, HD)
        return carry

    lax.fori_loop(0, 4, value_group, 0)
    attended = jnp.concatenate(
        [(att[h] + self_w[h] * v_f[h]).astype(BF) for h in range(2)], axis=1
    )

    for copy in ld_wout:
        copy.wait()
    for j in range(8):
        cts[j] = dot(attended, wout[j]).astype(BF)
    got_c = {
        k: push(
            cts.at[(me_h + k) % 8], ctr.at[me_h], cs_sem.at[k - 1], cr_sem.at[k - 1],
            (me_r, (me_h + k) % 8),
        )
        for k in order
    }
    ld_win.wait()
    relay_out(0, 16)
    total = hidden_ref[...].astype(F32) + cts[me_h].astype(F32)
    for k in (1, 7, 6, 2, 3, 5, 4):
        got_c[k].wait_recv()
        total = total + ctr[(me_h + 8 - k) % 8].astype(F32)
    resid[...] = total
    gath[z, c, y, x] = total.astype(BF)

    pl.semaphore_wait(cube_sem, 3)
    for dz in (0, 1, 3, 2):
        def send_rows(i, carry, dz=dz):
            remote(
                gath.at[z, c, y, x], gath.at[z, c, y, x], d_s, d_r.at[(4 - dz) % 4],
                at(i // 4, i % 4, dz),
            ).start()
            return carry

        lax.fori_loop(1 if dz == 0 else 0, 16, send_rows, 0)

    relay_out(16, 32)
    remote(
        kbuf.at[pl.ds(0, 15), pl.ds(0, ROWS)], kbuf.at[pl.ds(0, 15), pl.ds(0, ROWS)],
        t_s, t_r, other,
    ).wait_recv()

    def collect(g):
        zz = (z + g) % 4
        whole = yrecv.at[pl.ds(0, 15 if g == 0 else 16)]
        remote(whole, whole, d_s, d_r.at[g], other).wait_recv()
        return push(gath.at[zz, c], gath.at[zz, c], dd_s.at[g], dd_r.at[g], other)

    e_row = lax.broadcasted_iota(jnp.int32, (128, HD), 0)
    e_lane = lax.broadcasted_iota(jnp.int32, (128, HD), 1)

    def gate_up(group):
        m = 128 * len(group)
        scales, shares = [], []
        for i, g in enumerate(group):
            zz = (z + g) % 4
            part = None
            for j in range(8):
                block = gath[zz, j % 2, j // 2].reshape(128, 256)
                xs[128 * i : 128 * (i + 1), 256 * j : 256 * (j + 1)] = block
                f = block.astype(F32)
                f = f * f
                f = f[:, :128] + f[:, 128:]
                part = f if part is None else part + f
            mean = jnp.sum(part, axis=-1, keepdims=True) * (1.0 / D)
            scales.append(lax.rsqrt(mean + norm_eps))
            shares.append(tshare[zz].reshape(128, 128))
        scale = jnp.concatenate(scales, axis=0)
        shares = jnp.concatenate(shares, axis=0)
        low = lax.broadcasted_iota(jnp.int32, (m, HD), 1) < 64

        def body(n, carry):
            cols = pl.ds(pl.multiple_of(n * 256, 256), 256)
            got = dot(xs[:m, :], wrel[:, cols])
            pick = jnp.where(
                (e_row < 16) & ((e_row & 7) == 2 * n + (e_lane >> 6)), 1.0, 0.0
            ).astype(BF)
            share = dot(shares, pick)
            even = got[:, :128] * scale
            odd = got[:, 128:] * scale
            gate = jnp.where(low, even, pltpu.roll(odd, 64, 1))
            upward = jnp.where(low, pltpu.roll(even, 64, 1), odd)
            silu = gate / (1.0 + jnp.exp(-gate))
            units[:m, pl.ds(pl.multiple_of(n * 128, 128), 128)] = (
                share * (silu * upward)
            ).astype(BF)
            return carry

        lax.fori_loop(0, 4, body, 0)

    turns = (2, 1, 3, 0)
    got_x = {}

    def give(group):
        m = 128 * len(group)
        for dy in turns:
            val = dot(units[:m, :], wdown[((y + dy) % 4) * 2 + (1 - c)]).astype(BF)
            for i, g in enumerate(group):
                psend[g, dy] = val[128 * i : 128 * (i + 1)].reshape(4, ROWS, 256)
                got_x[g, dy] = push(
                    psend.at[g, dy], xrecv.at[g, dy], ps_s.at[g, dy], ps_r.at[g, dy], other
                )

    def keep(group):
        m = 128 * len(group)
        for dy in turns:
            val = dot(units[:m, :], wdown[((y + dy) % 4) * 2 + c])
            for i, g in enumerate(group):
                got_x[g, dy].wait_recv()
                mine = val[128 * i : 128 * (i + 1)] + xrecv[g, dy].reshape(128, 256).astype(F32)
                ssum[g, dy] = mine.astype(BF).reshape(4, ROWS, 256)

                def send_sum(dx, carry, dy=dy, g=g):
                    xx = (x + dx) % 4
                    slot = ((4 - g) % 4) * 16 + ((4 - dx) % 4) * 4 + (4 - dy) % 4
                    remote(
                        ssum.at[g, dy, xx], yrecv.at[slot], e_s, e_r.at[(4 - g) % 4],
                        at(dx, dy, g),
                    ).start()
                    return carry

                lax.fori_loop(1 if g == 0 and dy == 0 else 0, 4, send_sum, 0)

    for copy in ld_wdown:
        copy.wait()
    first = collect(0)
    first.wait_recv()
    gate_up((0,))
    give((0,))
    near = [collect(1), collect(3)]
    keep((0,))
    for copy in near:
        copy.wait_recv()
    gate_up((1, 3))
    give((1, 3))
    last = collect(2)
    keep((1, 3))
    last.wait_recv()
    gate_up((2,))
    give((2,))
    keep((2,))

    result = resid[...] + ssum[0, 0, x].astype(F32)
    for g in (0, 1, 3, 2):
        first_slot = 16 * g + (1 if g == 0 else 0)
        slots = pl.ds(first_slot, 15 if g == 0 else 16)
        remote(yrecv.at[slots], yrecv.at[slots], e_s, e_r.at[g], other).wait_recv()
        for i in range(first_slot, 16 * g + 16):
            result = result + yrecv[i].astype(F32)
    out_ref[...] = result.astype(BF)
    for copy in sends:
        copy.wait_send()
    cells = yrecv.at[pl.ds(1, 63)]
    remote(cells, cells, d_s, d_r.at[0], other).wait_send()
    remote(cells, cells, e_s, e_r.at[0], other).wait_send()
    few = kbuf.at[pl.ds(0, 15), pl.ds(0, ROWS)]
    remote(few, few, t_s, t_r, other).wait_send()


def layer(hidden, lengths, expert_ids, route_weights, w_qkv, w_out, k_cache, v_cache, w_in, w_down):
    half = HD // 2
    freqs = np.tile(rope_theta ** (-np.arange(half, dtype=np.float64) / half), 2)
    sign = np.repeat([-1.0, 1.0], half)

    vm = pl.BlockSpec(memory_space=pltpu.VMEM)
    hbm = pl.BlockSpec(memory_space=pl.ANY)
    V = pltpu.VMEM
    dma = pltpu.SemaphoreType.DMA
    regular = pltpu.SemaphoreType.REGULAR
    return pl.pallas_call(
        kernel,
        out_shape=jax.ShapeDtypeStruct((ROWS, 256), BF),
        in_specs=[vm] * 6 + [hbm] * 6,
        out_specs=vm,
        scratch_shapes=[
            V((3, 8, 256, 256), BF), V((8, 256, 256), BF), V((ROWS, COLS, HD), BF),
            V((ROWS, COLS, HD), BF), V((16384, 128), BF), V((2048, 1024), BF), V((8, 512, 256), BF),
            V((8, ROWS, 256), BF), V((2, ROWS, HD), F32), V((2, ROWS, COLS), F32),
            V((2, ROWS, HD), F32), V((8, ROWS, 256), BF), V((8, ROWS, 256), BF),
            V((ROWS, 256), F32), V((4, 2, 4, 4, ROWS, 256), BF), V((4, 4, ROWS, 128), BF),
            V((256, D), BF), V((256, 512), BF),
            V((4, 4, 4, ROWS, 256), BF), V((4, 4, 4, ROWS, 256), BF), V((4, 4, 4, ROWS, 256), BF),
            V((64, ROWS, 256), BF),
            dma((26,)), dma((7,)), dma((7,)), dma((7,)), dma((7,)), dma, dma, dma, dma((4,)),
            dma((4,)), dma((4,)), dma((4, 4)), dma((4, 4)), dma, dma((4,)), regular, regular,
        ],
        compiler_params=pltpu.CompilerParams(
            collective_id=0, has_side_effects=True, vmem_limit_bytes=60 * 1024 * 1024
        ),
    )(
        jnp.asarray(freqs.astype(np.float32)[None, :]), jnp.asarray(sign.astype(np.float32)[None, :]),
        hidden, lengths[None, :], expert_ids.T, route_weights.T,
        w_qkv.reshape(3, 8, 256, 256), w_out,
        k_cache.reshape(ROWS, COLS, HD), v_cache.reshape(ROWS, COLS, HD),
        w_in.reshape(16384, 128), w_down.reshape(512, D),
    )


def solution(mesh):
    in_specs = (
        P("req", "head"),
        P("req"),
        P("req", None),
        P("req", None),
        P(None, None, "head"),
        P("head", None),
        P("req", None, "head", None),
        P("req", None, "head", None),
        P(None, "head", "req"),
        P("head", "req", None),
    )
    return jax.shard_map(
        layer, mesh=mesh, in_specs=in_specs, out_specs=P("req", "head"), check_vma=False
    )
```

time: 296 us -> 60.6 us (0.20)
  the two profiles are of different devices: /device:TPU:0 before, /device:TPU:1 now
where the time goes in v2:
time: 60.6 us; the launch traced here: 60.4 us
  Pallas kernels  59 us (97%)
  local copies, waits for them, and re-layouts  1.32 us (2%)
    pallas_call x1, Pallas kernels, layer(): pl.pallas_call(kernel, out_shape=jax.ShapeDtypeStruct((ROWS, 256), BF), i...  59 us
    unnamed x1, local copies, waits for them, and re-layouts  1.32 us

profile of v2, /device:TPU:1, one launch (start us, length us, event | category | flops | bytes accessed | tf_op | source)
XLA Modules:
  0.0 60.4 jit_solution(9165316125164818069)
XLA Ops:
  0.0 59.0 %shard_map.118 = bf16[32,256]{1,0:T(8,128)(2,1)} custom-call(f32[1,128]{1,0:T(1,128)} %constant.4.clone.freq_ref, f32[1,128]{1,0:T(1,128)} %constant.5.clone.sign_ref, bf16[32,256]{1,0:T(8,128)(2,1)} %hidden_ref.1, s32[1,32]{1,0:T(1,128)} %bitcast.15, s32[8,32]{1,0:T(8,128)} %bitcast.13, f32[8,32]{1,0:T(8,128)} %bitcast.14, ...), custom_call_target="tpu_custom_call" | custom-call | tf_op jit(solution)/shard_map/pallas_call | solution.py:407
  59.0 1.3 %copy.14 = bf16[32,256]{1,0:T(8,128)(2,1)} copy(bf16[32,256]{1,0:T(8,128)(2,1)} %shard_map.118) | data formatting | bytes 32768

commit v3 on v2

--- a/solution.py
+++ b/solution.py
@@ -242,18 +242,17 @@
 
     for copy in ld_wout:
         copy.wait()
-    for j in range(8):
-        cts[j] = dot(attended, wout[j]).astype(BF)
-    got_c = {
-        k: push(
-            cts.at[(me_h + k) % 8], ctr.at[me_h], cs_sem.at[k - 1], cr_sem.at[k - 1],
-            (me_r, (me_h + k) % 8),
+    got_c = {}
+    for k in order:
+        peer = (me_h + k) % 8
+        cts[peer] = dot(attended, wout[peer]).astype(BF)
+        got_c[k] = push(
+            cts.at[peer], ctr.at[me_h], cs_sem.at[k - 1], cr_sem.at[k - 1], (me_r, peer)
         )
-        for k in order
-    }
+    mine = dot(attended, wout[me_h]).astype(BF).astype(F32)
     ld_win.wait()
     relay_out(0, 16)
-    total = hidden_ref[...].astype(F32) + cts[me_h].astype(F32)
+    total = hidden_ref[...].astype(F32) + mine
     for k in (1, 7, 6, 2, 3, 5, 4):
         got_c[k].wait_recv()
         total = total + ctr[(me_h + 8 - k) % 8].astype(F32)
@@ -261,8 +260,8 @@
     gath[z, c, y, x] = total.astype(BF)
 
     pl.semaphore_wait(cube_sem, 3)
-    for dz in (0, 1, 3, 2):
-        def send_rows(i, carry, dz=dz):
+    def spread(dz):
+        def send_rows(i, carry):
             remote(
                 gath.at[z, c, y, x], gath.at[z, c, y, x], d_s, d_r.at[(4 - dz) % 4],
                 at(i // 4, i % 4, dz),
@@ -271,7 +270,11 @@
 
         lax.fori_loop(1 if dz == 0 else 0, 16, send_rows, 0)
 
-    relay_out(16, 32)
+    spread(2)
+    relay_out(16, 24)
+    spread(1)
+    spread(3)
+    relay_out(24, 32)
     remote(
         kbuf.at[pl.ds(0, 15), pl.ds(0, ROWS)], kbuf.at[pl.ds(0, 15), pl.ds(0, ROWS)],
         t_s, t_r, other,
@@ -360,25 +363,26 @@
 
     for copy in ld_wdown:
         copy.wait()
-    first = collect(0)
+    first = collect(2)
+    spread(0)
     first.wait_recv()
-    gate_up((0,))
-    give((0,))
+    gate_up((2,))
+    give((2,))
     near = [collect(1), collect(3)]
-    keep((0,))
+    keep((2,))
     for copy in near:
         copy.wait_recv()
     gate_up((1, 3))
     give((1, 3))
-    last = collect(2)
+    last = collect(0)
     keep((1, 3))
     last.wait_recv()
-    gate_up((2,))
-    give((2,))
-    keep((2,))
+    gate_up((0,))
+    give((0,))
+    keep((0,))
 
     result = resid[...] + ssum[0, 0, x].astype(F32)
-    for g in (0, 1, 3, 2):
+    for g in (2, 1, 3, 0):
         first_slot = 16 * g + (1 if g == 0 else 0)
         slots = pl.ds(first_slot, 15 if g == 0 else 16)
         remote(yrecv.at[slots], yrecv.at[slots], e_s, e_r.at[g], other).wait_recv()

time: 60.6 us -> 58.4 us (0.964)
  the two profiles are of different devices: /device:TPU:1 before, /device:TPU:0 now
where the time goes in v3:
time: 58.4 us; the launch traced here: 58.2 us
  Pallas kernels  56.9 us (97%)
  local copies, waits for them, and re-layouts  1.32 us (2%)
    pallas_call x1, Pallas kernels, layer(): pl.pallas_call(kernel, out_shape=jax.ShapeDtypeStruct((ROWS, 256), BF), i...  56.9 us
    unnamed x1, local copies, waits for them, and re-layouts  1.32 us

profile of v3, /device:TPU:0, one launch (start us, length us, event | category | flops | bytes accessed | tf_op | source)
XLA Modules:
  0.0 58.2 jit_solution(3214184367442638070)
XLA Ops:
  0.0 56.9 %shard_map.118 = bf16[32,256]{1,0:T(8,128)(2,1)} custom-call(f32[1,128]{1,0:T(1,128)} %constant.4.clone.freq_ref, f32[1,128]{1,0:T(1,128)} %constant.5.clone.sign_ref, bf16[32,256]{1,0:T(8,128)(2,1)} %hidden_ref.1, s32[1,32]{1,0:T(1,128)} %bitcast.15, s32[8,32]{1,0:T(8,128)} %bitcast.13, f32[8,32]{1,0:T(8,128)} %bitcast.14, ...), custom_call_target="tpu_custom_call" | custom-call | tf_op jit(solution)/shard_map/pallas_call | solution.py:411
  56.9 1.3 %copy.14 = bf16[32,256]{1,0:T(8,128)(2,1)} copy(bf16[32,256]{1,0:T(8,128)(2,1)} %shard_map.118) | data formatting | bytes 32768
